TPU v7x, 128 devices: a whole 4x4x4 slice. The times are simulated.
128 devices in a mesh: grid: 32 (over z, x, core), rep: 4 (over y).
Axes of the slice: x: 4, y: 4, z: 4, core: 2. Of those that a mesh axis runs over, the one named last changes fastest.
Arguments:
- functions: bfloat16 [8192, 32768], P(('grid', 'rep')), may hold values from -6 to 6
- filter_taps: bfloat16 [16], replicated, may hold values from -0.59765625 to 0.59765625
- potential: float32 [32768], replicated, may hold values from 0 to 1
- energies: float32 [8192], P(('grid', 'rep')), may hold values from -1.5 to -0.5
- region_start: int32 [8192], P(('grid', 'rep')), may hold values from 0 to 128
- region_length: int32 [8192], P(('grid', 'rep')), may hold values from 256 to 384
- partner_groups: int32 [128, 3], replicated, may hold values from 0 to 127, as said below
Outputs:
- corrected: bfloat16 [8192, 32768], P(('grid', 'rep'))
Inputs may be any that keep to these rules, and one draw needn't show every extreme that they name: `partner_groups`: the 3 entries of a row are distinct and differ from the row's own group; each is the row's group plus an offset of magnitude 1 to 63, modulo 128.
All inputs are finite; a program needn't handle non-finite values.
Results may differ from a plain program's by a relative error of at most 0.005.
Values may be sent and summed in bfloat16 or wider, within the bound.
A program may use at most 128 MiB of HBM per device.

v0:
```python
import jax
import jax.numpy as jnp
from jax import lax
from jax.sharding import PartitionSpec as P

SIDE = 32
NC = 32768
BLOCK = 64
GROUP = 64
TAPS = 16
PARTNERS = 3
LMAX = 384


def filter_matrix(filter_taps, extent):
    centre = TAPS // 2
    inputs = jnp.arange(extent, dtype=jnp.int32)
    distance = inputs[:, None] - inputs[None, :] + centre
    choose = (distance[:, :, None] == jnp.arange(TAPS, dtype=jnp.int32)[None, None, :]).astype(
        jnp.float32
    )
    return jnp.sum(choose * filter_taps.astype(jnp.float32)[None, None, :], axis=2)


def on_device(
    functions, filter_taps, potential, energies, region_start, region_length, partner_groups
):
    count_rows = functions.shape[0]
    grid_size = lax.axis_size("grid")
    rep_size = lax.axis_size("rep")
    devices_all = grid_size * rep_size
    local_cols = NC // devices_all
    single = filter_matrix(filter_taps, SIDE)
    ident = jnp.eye(SIDE, dtype=jnp.float32)
    plane_matrix = (jnp.kron(single, ident) + jnp.kron(ident, single)).astype(jnp.bfloat16)
    line_matrix = single.astype(jnp.bfloat16)
    slabs = functions.reshape(count_rows, SIDE, SIDE * SIDE)
    plane_part = jnp.dot(
        functions.reshape(count_rows * SIDE, SIDE * SIDE),
        plane_matrix,
        preferred_element_type=jnp.float32,
    ).reshape(count_rows, SIDE, SIDE * SIDE)
    line_part = jnp.einsum("fxc,xw->fwc", slabs, line_matrix, preferred_element_type=jnp.float32)
    kinetic = (plane_part + line_part).reshape(count_rows, NC)
    values = functions.astype(jnp.float32)
    gradient = kinetic + potential[None, :] * values - energies[:, None] * values
    updated = values - 0.3 * gradient / (1.0 - energies)[:, None]
    block_index = jnp.arange(NC, dtype=jnp.int32) // BLOCK
    inside = (block_index[None, :] >= region_start[:, None]) & (
        block_index[None, :] < (region_start + region_length)[:, None]
    )
    refined = jnp.where(inside, updated, 0.0).astype(jnp.bfloat16)
    gridded = lax.all_to_all(refined, ("grid", "rep"), split_axis=1, concat_axis=0, tiled=True)
    group_count = gridded.shape[0] // GROUP
    grouped = gridded.reshape(group_count, GROUP, local_cols)
    partner_rows = grouped[partner_groups]
    stacked = jnp.concatenate([grouped[:, None], partner_rows], axis=1)
    local_intersection = jnp.einsum(
        "agc,akhc->akgh", grouped, stacked, preferred_element_type=jnp.float32
    )
    weight = 1.0 / (BLOCK * LMAX)
    identity_block = jnp.concatenate(
        [jnp.eye(GROUP, dtype=jnp.float32)[None], jnp.zeros((PARTNERS, GROUP, GROUP), jnp.float32)],
        axis=0,
    )
    summed = lax.psum(local_intersection, ("grid", "rep"))
    coupling = (0.5 * (summed * weight - identity_block[None])).astype(jnp.bfloat16)
    shifted = jnp.einsum("akgh,akhc->agc", coupling, stacked, preferred_element_type=jnp.float32)
    result_grid = (grouped.astype(jnp.float32) - shifted).astype(jnp.bfloat16)
    result_grid = result_grid.reshape(group_count * GROUP, local_cols)
    return lax.all_to_all(result_grid, ("grid", "rep"), split_axis=0, concat_axis=1, tiled=True)


def solution(mesh):
    return jax.shard_map(
        on_device,
        mesh=mesh,
        in_specs=(
            P(("grid", "rep"), None),
            P(),
            P(),
            P(("grid", "rep")),
            P(("grid", "rep")),
            P(("grid", "rep")),
            P(),
        ),
        out_specs=P(("grid", "rep"), None),
        check_vma=False,
    )
```

profile of v0, /device:TPU:1, one launch (start us, length us, event | category | flops | bytes accessed | tf_op | source)
XLA Modules:
  0.0 433.5 jit_solution(11363357073585440919)
XLA Ops:
  6.6 0.7 convert_element_type.56
  7.2 0.1 select_reduce_fusion
  7.4 5.9 %add_convert_fusion = bf16[32,32,32,32]{3,2,1,0:T(8,128)(2,1)} fusion(f32[32,32]{1,0:T(8,128)S(1)} %select_reduce_fusion, f32[32,32]{1,0:T(8,128)S(1)} %fusion.13), kind=kLoop, calls=%fused_computation.2 | loop fusion | flops 4194304 | bytes 2105344 | tf_op jit(solution)/shard_map/convert_element_type | solution.py:35
  13.3 11.3 %convert_element_type.59 = bf16[1024,1024]{1,0:T(8,128)(2,1)S(1)} reshape(bf16[32,32,32,32]{3,2,1,0:T(8,128)(2,1)} %add_convert_fusion) | data formatting | bytes 4194304 | tf_op jit(solution)/shard_map/convert_element_type | solution.py:35
  24.6 7.4 %reshape.111 = bf16[2048,1024]{1,0:T(8,128)(2,1)} reshape(bf16[64,32768]{1,0:T(8,128)(2,1)} %param.7) | data formatting | bytes 8388608 | tf_op jit(solution)/shard_map/reshape | solution.py:39
  32.0 9.0 %convolution_bitcast_fusion = f32[2048,1024]{0,1:T(8,128)} fusion(bf16[1024,1024]{1,0:T(8,128)(2,1)S(1)} %convert_element_type.59, bf16[2048,1024]{1,0:T(8,128)(2,1)} %reshape.111), kind=kOutput, calls=%fused_computation.18 | convolution fusion | flops 4294967296 | bytes 14680064 | tf_op jit(solution)/shard_map/dot_general | solution.py:38
  41.0 9.2 %copy.24 = f32[2048,1024]{1,0:T(8,128)} copy(f32[2048,1024]{0,1:T(8,128)} %convolution_bitcast_fusion) | data formatting | bytes 16777216 | tf_op jit(solution)/shard_map/dot_general | solution.py:38
  50.2 0.0 copy-start.1
  50.2 4.8 %copy.38 = bf16[8,8,32,1024]{3,2,1,0:T(8,128)(2,1)S(1)} copy(bf16[8,8,32,1024]{3,1,2,0:T(8,128)(2,1)} %bitcast.44) | data formatting | bytes 8388608
  55.0 0.0 copy-done.1
  55.0 1.3 bitcast_add_fusion
  56.3 0.0 copy-start.4
  56.3 0.0 copy-start.5
  56.3 0.0 copy-start.6
  56.3 0.0 copy-start
  56.4 0.0 copy-start.2
  56.4 5.0 %copy.39 = f32[8,8,32,1024]{3,1,2,0:T(8,128)S(1)} copy(f32[8,8,32,1024]{3,2,1,0:T(8,128)S(1)} %bitcast.48) | data formatting | bytes 16777216
  61.4 0.0 copy-done.4
  61.4 0.0 copy-done.5
  61.5 0.0 copy-done.6
  61.5 0.0 copy-done
  61.5 0.0 copy-done.2
  61.5 3.5 fusion.8
  65.0 0.0 copy-start.3
  65.1 2.6 copy.41
  67.6 11.9 %all-to-all-start = ((bf16[64,128,256]{2,0,1:T(8,128)(2,1)}), bf16[64,128,256]{2,0,1:T(8,128)(2,1)}, u32[]{:S(2)}, u32[]{:S(2)}) async-start(bf16[64,128,256]{2,0,1:T(8,128)(2,1)} %bitcast.50), calls=%async_computation | async-start | bytes 8388608 | tf_op jit(solution)/shard_map/all_to_all | solution.py:53
  79.6 0.3 all-reduce.3.cloned.1.call-start
  79.9 0.0 copy-done.3
  79.9 0.1 copy.27
  80.0 0.2 reshape.117
  80.2 52.2 %all-to-all-done = bf16[64,128,256]{2,0,1:T(8,128)(2,1)} async-done(((bf16[64,128,256]{2,0,1:T(8,128)(2,1)}), bf16[64,128,256]{2,0,1:T(8,128)(2,1)}, u32[]{:S(2)}, u32[]{:S(2)}) %all-to-all-start) | async-done | bytes 4194336 | tf_op jit(solution)/shard_map/all_to_all | solution.py:53
  132.4 13.5 %gather_fusion = bf16[384,64,256]{2,1,0:T(8,128)(2,1)} fusion(bf16[128,64,256]{2,1,0:T(8,128)(2,1)} %bitcast.4, s32[1024]{0:T(1024)S(1)} %pad_clamp_fusion), kind=kCustom, calls=%fused_computation | custom fusion | bytes 25167360 | tf_op jit(solution)/shard_map/gather | solution.py:56
  145.9 12.7 %fusion.1 = f32[128,4,64,64]{3,2,1,0:T(8,128)} fusion(bf16[128,3,64,256]{3,2,1,0:T(8,128)(2,1)} %bitcast.53, bf16[128,1,64,256]{3,2,1,0:T(8,128)(2,1)} %bitcast.6, bf16[64,128,256]{2,0,1:T(8,128)(2,1)} %all-to-all-done), kind=kOutput, calls=%fused_computation.7 | convolution fusion | flops 1082130432 | bytes 29360128 | tf_op jit(solution)/shard_map/agc,akhc->akgh/dot_general | solution.py:58
  158.6 15.7 %copy.29 = f32[128,4,64,64]{0,2,3,1:T(8,128)} copy(f32[128,4,64,64]{3,2,1,0:T(8,128)} %fusion.1) | data formatting | bytes 16777216 | tf_op jit(solution)/shard_map/agc,akhc->akgh/dot_general | solution.py:58
  174.4 0.0 all-reduce.3.cloned.1.call-update
  174.4 157.0 %all-reduce.3.cloned.1.call-done = f32[128,4,64,64]{0,3,2,1:T(8,128)} async-done(((f32[128,4,64,64]{0,3,2,1:T(8,128)}), f32[128,4,64,64]{0,3,2,1:T(8,128)}) %all-reduce.3.cloned.1.call-update) | async-done | bytes 8388624 | tf_op jit(solution)/shard_map/psum | solution.py:66
  331.4 6.8 %multiply_convert_fusion = bf16[128,4,64,64]{0,3,2,1:T(8,128)(2,1)} fusion(f32[128,4,64,64]{0,3,2,1:T(8,128)} %all-reduce.3.cloned.1.call-done, f32[4,64,64]{2,1,0:T(8,128)S(1)} %pad_convert_fusion), kind=kLoop, calls=%fused_computation.16 | loop fusion | flops 8388608 | bytes 12648448 | tf_op jit(solution)/shard_map/convert_element_type | solution.py:67
  338.2 12.9 %copy.30 = bf16[128,4,64,64]{3,2,1,0:T(8,128)(2,1)} copy(bf16[128,4,64,64]{0,3,2,1:T(8,128)(2,1)} %multiply_convert_fusion) | data formatting | bytes 8388608 | tf_op jit(solution)/shard_map/convert_element_type | solution.py:67
  351.2 13.1 %fusion.7 = bf16[128,64,256]{2,1,0:T(8,128)(2,1)} fusion(bf16[128,4,64,64]{3,2,1,0:T(8,128)(2,1)} %copy.30, bf16[128,3,64,256]{3,2,1,0:T(8,128)(2,1)} %bitcast.54, bf16[128,1,64,256]{3,2,1,0:T(8,128)(2,1)} %bitcast.6, bf16[64,128,256]{2,0,1:T(8,128)(2,1)} %all-to-all-done), kind=kOutput, calls=%fused_computation.14 | convolution fusion | flops 1088421888 | bytes 29360128 | tf_op jit(solution)/shard_map/akgh,akhc->agc/dot_general | solution.py:68
  364.3 60.1 %all_to_all.32 = bf16[128,64,256]{2,1,0:T(8,128)(2,1)S(1)} all-to-all(bf16[128,64,256]{2,1,0:T(8,128)(2,1)} %fusion.7), channel_id=1, replica_groups=mesh['grid'=32,'rep'=4] {'grid','rep'}, dimensions={0} | all-to-all | bytes 8388608 | tf_op jit(solution)/shard_map/all_to_all | solution.py:71
  424.3 2.3 copy.37
  (9 shorter events, 0.1 us)
Async XLA Ops:
  50.2 4.8 %copy-start.1 = (f32[2048,1024]{1,0:T(8,128)S(1)}, f32[2048,1024]{1,0:T(8,128)}, u32[]{:S(2)}) copy-start(f32[2048,1024]{1,0:T(8,128)} %copy.24) | copy-start | bytes 25165828
  56.3 5.1 %copy-start.4 = (f32[64]{0:T(128)S(1)}, f32[64]{0:T(128)}, u32[]{:S(2)}) copy-start(f32[64]{0:T(128)} %param.10) | copy-start | bytes 772
  56.3 5.1 %copy-start.5 = (s32[64]{0:T(128)S(1)}, s32[64]{0:T(128)}, u32[]{:S(2)}) copy-start(s32[64]{0:T(128)} %param.11) | copy-start | bytes 772
  56.3 5.1 %copy-start.6 = (s32[64]{0:T(128)S(1)}, s32[64]{0:T(128)}, u32[]{:S(2)}) copy-start(s32[64]{0:T(128)} %param.12) | copy-start | bytes 772
  56.3 5.1 %copy-start = (bf16[64,32768]{1,0:T(8,128)(2,1)S(1)}, bf16[64,32768]{1,0:T(8,128)(2,1)}, u32[]{:S(2)}) copy-start(bf16[64,32768]{1,0:T(8,128)(2,1)} %param.7) | copy-start | bytes 12582916
  56.4 5.1 %copy-start.2 = (f32[32768]{0:T(1024)S(1)}, f32[32768]{0:T(1024)}, u32[]{:S(2)}) copy-start(f32[32768]{0:T(1024)} %param.9) | copy-start | bytes 393220
  65.0 14.8 %copy-start.3 = (s32[128,3]{0,1:T(4,128)S(1)}, s32[128,3]{0,1:T(4,128)}, u32[]{:S(2)}) copy-start(s32[128,3]{0,1:T(4,128)} %param.13) | copy-start | bytes 4612
  67.6 64.8 %all-to-all-start = ((bf16[64,128,256]{2,0,1:T(8,128)(2,1)}), bf16[64,128,256]{2,0,1:T(8,128)(2,1)}, u32[]{:S(2)}, u32[]{:S(2)}) async-start(bf16[64,128,256]{2,0,1:T(8,128)(2,1)} %bitcast.50), calls=%async_computation | async-start | bytes 8388608 | tf_op jit(solution)/shard_map/all_to_all | solution.py:53
  79.6 251.8 %all-reduce.3.cloned.1.call-start = ((), (), s32[]{:S(2)}) async-start(), calls=%async_computation.2 | async-start | bytes 16777216 | tf_op jit(solution)/shard_map/psum | solution.py:66
Sparse Core Ops, SparseCore 0:
  174.5 156.8 all-reduce.2
where the time goes:
time: 435 us; the launch traced here: 433 us
  waiting for transfers between devices  209 us (48%)
  local copies, waits for them, and re-layouts  85.2 us (20%)
  blocking collectives  60.1 us (14%)
  matrix products  36.1 us (8%)
  other arithmetic  17.1 us (4%)
  between operations  13.6 us (3%)
  starting transfers between devices  12.2 us (3%)
    psum x1, waiting for transfers between devices, on_device(): summed = lax.psum(local_intersection, ('grid', 'rep'))  157 us
    all_to_all x1, blocking collectives, on_device(): lax.all_to_all(result_grid, ('grid', 'rep'), split_axis=0, concat_axis=1,...  60.1 us
    all_to_all x1, waiting for transfers between devices, on_device(): lax.all_to_all(refined, ('grid', 'rep'), split_axis=1, concat_axis=0, til...  52.2 us
    dot_general x1, local copies, waits for them, and re-layouts, on_device(): jnp.einsum('agc,akhc->akgh', grouped, stacked, preferred_element_type=jnp...  15.7 us
    gather x1, local copies, waits for them, and re-layouts, on_device(): partner_rows = grouped[partner_groups]  13.5 us
    dot_general x1, matrix products, on_device(): jnp.einsum('akgh,akhc->agc', coupling, stacked, preferred_element_type=jn...  13.1 us
    convert_element_type x1, local copies, waits for them, and re-layouts, on_device(): (0.5 * (summed * weight - identity_block[None])).astype(jnp.bfloat16)  12.9 us
    dot_general x1, matrix products, on_device(): jnp.einsum('agc,akhc->akgh', grouped, stacked, preferred_element_type=jnp...  12.7 us
  transfers between devices with their start and end apart: 2, of which 2 were waited for; matrix products, arithmetic and copies ran while one was open for 0% of the time, Pallas kernels for 0%

commit v1 on v0

--- a/solution.py
+++ b/solution.py
@@ -63,7 +63,7 @@
         [jnp.eye(GROUP, dtype=jnp.float32)[None], jnp.zeros((PARTNERS, GROUP, GROUP), jnp.float32)],
         axis=0,
     )
-    summed = lax.psum(local_intersection, ("grid", "rep"))
+    summed = lax.psum(lax.psum(local_intersection, "rep"), "grid")
     coupling = (0.5 * (summed * weight - identity_block[None])).astype(jnp.bfloat16)
     shifted = jnp.einsum("akgh,akhc->agc", coupling, stacked, preferred_element_type=jnp.float32)
     result_grid = (grouped.astype(jnp.float32) - shifted).astype(jnp.bfloat16)

time: 435 us -> 558 us (1.28)
  waiting for transfers between devices: 209 us -> 332 us
    psum x1 -> x2, waiting for transfers between devices: 157 us -> 279 us  [on_device(): summed = lax.psum(lax.psum(local_intersection, 'rep'), 'grid')]
  transfers between devices with their start and end apart: 2 -> 3, of which waited for: 2 -> 3; matrix products, arithmetic and copies ran while one was open for 0% -> 0% of each run, Pallas kernels for 0% -> 0%
where the time goes in v1:
time: 558 us; the launch traced here: 557 us
  waiting for transfers between devices  332 us (59%)
  local copies, waits for them, and re-layouts  85.2 us (15%)
  blocking collectives  61.1 us (11%)
  matrix products  36.1 us (6%)
  other arithmetic  17.1 us (3%)
  between operations  13.6 us (2%)
  starting transfers between devices  12.2 us (2%)
    psum x2, waiting for transfers between devices, on_device(): summed = lax.psum(lax.psum(local_intersection, 'rep'), 'grid')  279 us
    all_to_all x1, blocking collectives, on_device(): lax.all_to_all(result_grid, ('grid', 'rep'), split_axis=0, concat_axis=1,...  61.1 us
    all_to_all x1, waiting for transfers between devices, on_device(): lax.all_to_all(refined, ('grid', 'rep'), split_axis=1, concat_axis=0, til...  52.2 us
    dot_general x1, local copies, waits for them, and re-layouts, on_device(): jnp.einsum('agc,akhc->akgh', grouped, stacked, preferred_element_type=jnp...  15.7 us
    gather x1, local copies, waits for them, and re-layouts, on_device(): partner_rows = grouped[partner_groups]  13.5 us
    dot_general x1, matrix products, on_device(): jnp.einsum('akgh,akhc->agc', coupling, stacked, preferred_element_type=jn...  13.1 us
    convert_element_type x1, local copies, waits for them, and re-layouts, on_device(): (0.5 * (summed * weight - identity_block[None])).astype(jnp.bfloat16)  12.9 us
    dot_general x1, matrix products, on_device(): jnp.einsum('agc,akhc->akgh', grouped, stacked, preferred_element_type=jnp...  12.7 us
  transfers between devices with their start and end apart: 3, of which 3 were waited for; matrix products, arithmetic and copies ran while one was open for 0% of the time, Pallas kernels for 0%

profile of v1, /device:TPU:1, one launch (start us, length us, event | category | flops | bytes accessed | tf_op | source)
XLA Modules:
  0.0 556.9 jit_solution(17999985867652524109)
XLA Ops:
  6.6 0.7 convert_element_type.56
  7.2 0.1 select_reduce_fusion
  7.4 5.9 %add_convert_fusion = bf16[32,32,32,32]{3,2,1,0:T(8,128)(2,1)} fusion(f32[32,32]{1,0:T(8,128)S(1)} %select_reduce_fusion, f32[32,32]{1,0:T(8,128)S(1)} %fusion.13), kind=kLoop, calls=%fused_computation.2 | loop fusion | flops 4194304 | bytes 2105344 | tf_op jit(solution)/shard_map/convert_element_type | solution.py:35
  13.3 11.3 %convert_element_type.59 = bf16[1024,1024]{1,0:T(8,128)(2,1)S(1)} reshape(bf16[32,32,32,32]{3,2,1,0:T(8,128)(2,1)} %add_convert_fusion) | data formatting | bytes 4194304 | tf_op jit(solution)/shard_map/convert_element_type | solution.py:35
  24.6 7.4 %reshape.111 = bf16[2048,1024]{1,0:T(8,128)(2,1)} reshape(bf16[64,32768]{1,0:T(8,128)(2,1)} %param.7) | data formatting | bytes 8388608 | tf_op jit(solution)/shard_map/reshape | solution.py:39
  32.0 9.0 %convolution_bitcast_fusion = f32[2048,1024]{0,1:T(8,128)} fusion(bf16[1024,1024]{1,0:T(8,128)(2,1)S(1)} %convert_element_type.59, bf16[2048,1024]{1,0:T(8,128)(2,1)} %reshape.111), kind=kOutput, calls=%fused_computation.18 | convolution fusion | flops 4294967296 | bytes 14680064 | tf_op jit(solution)/shard_map/dot_general | solution.py:38
  41.0 9.2 %copy.24 = f32[2048,1024]{1,0:T(8,128)} copy(f32[2048,1024]{0,1:T(8,128)} %convolution_bitcast_fusion) | data formatting | bytes 16777216 | tf_op jit(solution)/shard_map/dot_general | solution.py:38
  50.2 0.0 copy-start.1
  50.2 4.8 copy.38
  55.0 0.0 copy-done.1
  55.0 1.3 bitcast_add_fusion
  56.3 0.0 copy-start.4
  56.3 0.0 copy-start.5
  56.3 0.0 copy-start.6
  56.3 0.0 copy-start
  56.4 0.0 copy-start.2
  56.4 5.0 copy.39
  61.4 0.0 copy-done.4
  61.4 0.0 copy-done.5
  61.5 0.0 copy-done.6
  61.5 0.0 copy-done
  61.5 0.0 copy-done.2
  61.5 3.5 fusion.8
  65.0 0.0 copy-start.3
  65.1 2.6 copy.41
  67.6 11.9 %all-to-all-start = ((bf16[64,128,256]{2,0,1:T(8,128)(2,1)}), bf16[64,128,256]{2,0,1:T(8,128)(2,1)}, u32[]{:S(2)}, u32[]{:S(2)}) async-start(bf16[64,128,256]{2,0,1:T(8,128)(2,1)} %bitcast.50), calls=%async_computation | async-start | bytes 8388608 | tf_op jit(solution)/shard_map/all_to_all | solution.py:53
  79.6 0.3 all-reduce.4.cloned.1.call-start
  79.9 0.0 copy-done.3
  79.9 0.1 copy.27
  80.0 0.2 reshape.117
  80.2 52.2 %all-to-all-done = bf16[64,128,256]{2,0,1:T(8,128)(2,1)} async-done(((bf16[64,128,256]{2,0,1:T(8,128)(2,1)}), bf16[64,128,256]{2,0,1:T(8,128)(2,1)}, u32[]{:S(2)}, u32[]{:S(2)}) %all-to-all-start) | async-done | bytes 4194336 | tf_op jit(solution)/shard_map/all_to_all | solution.py:53
  132.4 13.5 %gather_fusion = bf16[384,64,256]{2,1,0:T(8,128)(2,1)} fusion(bf16[128,64,256]{2,1,0:T(8,128)(2,1)} %bitcast.4, s32[1024]{0:T(1024)S(1)} %pad_clamp_fusion), kind=kCustom, calls=%fused_computation | custom fusion | bytes 25167360 | tf_op jit(solution)/shard_map/gather | solution.py:56
  145.9 12.7 %fusion.1 = f32[128,4,64,64]{3,2,1,0:T(8,128)} fusion(bf16[128,3,64,256]{3,2,1,0:T(8,128)(2,1)} %bitcast.53, bf16[128,1,64,256]{3,2,1,0:T(8,128)(2,1)} %bitcast.6, bf16[64,128,256]{2,0,1:T(8,128)(2,1)} %all-to-all-done), kind=kOutput, calls=%fused_computation.7 | convolution fusion | flops 1082130432 | bytes 29360128 | tf_op jit(solution)/shard_map/agc,akhc->akgh/dot_general | solution.py:58
  158.6 15.7 %copy.29 = f32[128,4,64,64]{0,2,3,1:T(8,128)} copy(f32[128,4,64,64]{3,2,1,0:T(8,128)} %fusion.1) | data formatting | bytes 16777216 | tf_op jit(solution)/shard_map/agc,akhc->akgh/dot_general | solution.py:58
  174.4 0.0 all-reduce.4.cloned.1.call-update
  174.4 0.0 all-reduce.6.cloned.1.call-start
  174.4 155.7 %all-reduce.4.cloned.1.call-done = f32[128,4,64,64]{0,3,2,1:T(8,128)} async-done(((f32[128,4,64,64]{0,3,2,1:T(8,128)}), f32[128,4,64,64]{0,3,2,1:T(8,128)}) %all-reduce.4.cloned.1.call-update) | async-done | bytes 8388624 | tf_op jit(solution)/shard_map/psum | solution.py:66
  330.2 0.0 all-reduce.6.cloned.1.call-update
  330.3 123.5 %all-reduce.6.cloned.1.call-done = f32[128,4,64,64]{0,3,2,1:T(8,128)} async-done(((f32[128,4,64,64]{0,3,2,1:T(8,128)}), f32[128,4,64,64]{0,3,2,1:T(8,128)}) %all-reduce.6.cloned.1.call-update) | async-done | bytes 8388624 | tf_op jit(solution)/shard_map/psum | solution.py:66
  453.8 6.8 %multiply_convert_fusion = bf16[128,4,64,64]{0,3,2,1:T(8,128)(2,1)} fusion(f32[128,4,64,64]{0,3,2,1:T(8,128)} %all-reduce.6.cloned.1.call-done, f32[4,64,64]{2,1,0:T(8,128)S(1)} %pad_convert_fusion), kind=kLoop, calls=%fused_computation.16 | loop fusion | flops 8388608 | bytes 12648448 | tf_op jit(solution)/shard_map/convert_element_type | solution.py:67
  460.6 12.9 %copy.30 = bf16[128,4,64,64]{3,2,1,0:T(8,128)(2,1)} copy(bf16[128,4,64,64]{0,3,2,1:T(8,128)(2,1)} %multiply_convert_fusion) | data formatting | bytes 8388608 | tf_op jit(solution)/shard_map/convert_element_type | solution.py:67
  473.6 13.1 %fusion.7 = bf16[128,64,256]{2,1,0:T(8,128)(2,1)} fusion(bf16[128,4,64,64]{3,2,1,0:T(8,128)(2,1)} %copy.30, bf16[128,3,64,256]{3,2,1,0:T(8,128)(2,1)} %bitcast.54, bf16[128,1,64,256]{3,2,1,0:T(8,128)(2,1)} %bitcast.6, bf16[64,128,256]{2,0,1:T(8,128)(2,1)} %all-to-all-done), kind=kOutput, calls=%fused_computation.14 | convolution fusion | flops 1088421888 | bytes 29360128 | tf_op jit(solution)/shard_map/akgh,akhc->agc/dot_general | solution.py:68
  486.6 61.1 %all_to_all.32 = bf16[128,64,256]{2,1,0:T(8,128)(2,1)S(1)} all-to-all(bf16[128,64,256]{2,1,0:T(8,128)(2,1)} %fusion.7), channel_id=1, replica_groups=mesh['grid'=32,'rep'=4] {'grid','rep'}, dimensions={0} | all-to-all | bytes 8388608 | tf_op jit(solution)/shard_map/all_to_all | solution.py:71
  547.8 2.3 copy.37
  (9 shorter events, 0.1 us)
Async XLA Ops:
  50.2 4.8 copy-start.1
  56.3 5.1 copy-start.4
  56.3 5.1 copy-start.5
  56.3 5.1 copy-start.6
  56.3 5.1 copy-start
  56.4 5.1 copy-start.2
  65.0 14.8 %copy-start.3 = (s32[128,3]{0,1:T(4,128)S(1)}, s32[128,3]{0,1:T(4,128)}, u32[]{:S(2)}) copy-start(s32[128,3]{0,1:T(4,128)} %param.13) | copy-start | bytes 4612
  67.6 64.8 %all-to-all-start = ((bf16[64,128,256]{2,0,1:T(8,128)(2,1)}), bf16[64,128,256]{2,0,1:T(8,128)(2,1)}, u32[]{:S(2)}, u32[]{:S(2)}) async-start(bf16[64,128,256]{2,0,1:T(8,128)(2,1)} %bitcast.50), calls=%async_computation | async-start | bytes 8388608 | tf_op jit(solution)/shard_map/all_to_all | solution.py:53
  79.6 250.6 %all-reduce.4.cloned.1.call-start = ((), (), s32[]{:S(2)}) async-start(), calls=%async_computation.2 | async-start | bytes 16777216 | tf_op jit(solution)/shard_map/psum | solution.py:66
  174.4 279.4 %all-reduce.6.cloned.1.call-start = ((), (), s32[]{:S(2)}) async-start(), calls=%async_computation.3 | async-start | bytes 16777216 | tf_op jit(solution)/shard_map/psum | solution.py:66
Sparse Core Ops, SparseCore 0:
  174.5 155.6 all-reduce.3
  333.6 120.1 all-reduce.5
